TPU v7x, 256 devices: a whole 4x4x8 slice. The times are simulated.
256 devices in a mesh: dp: 2 (over x_lo), expert: 8 (over z), shard: 16 (over x_hi, y, core).
Axes of the slice: x: 4 (x_hi: 2, x_lo: 2; x = x_hi * 2 + x_lo), y: 4, z: 8, core: 2. Of those that a mesh axis runs over, the one named last changes fastest.
Arguments:
- tokens: bfloat16 [2048, 6144], P(('dp', 'expert', 'shard')), may hold values from -6 to 6
- gate_up_weight: bfloat16 [8, 2, 8192, 6144], P(None, None, ('dp', 'expert', 'shard')), may hold values from -0.078125 to 0.078125
- down_weight: bfloat16 [8, 8192, 6144], P(None, ('dp', 'expert', 'shard')), may hold values from -0.0625 to 0.0625
- expert_ids: int32 [2048, 2], P(('dp', 'expert', 'shard')), may hold values from 0 to 7, as said below
- slot_ids: int32 [2048, 2], P(('dp', 'expert', 'shard')), may hold values from 0 to 3, as said below
- gate_values: float32 [2048, 2], P(('dp', 'expert', 'shard')), may hold values from 0.1 to 1
- old_place: int32 [8], replicated, may hold values from 0 to 7, each once
- new_place: int32 [8], replicated, may hold values from 0 to 7, each once
Outputs:
- mixed_out: bfloat16 [2048, 6144], P(('dp', 'expert', 'shard'))
Inputs may be any that keep to these rules, and one draw needn't show every extreme that they name: `expert_ids`: each token names 2 different experts; among the 8 tokens of one block no expert is named more than 4 times, and one expert is named exactly 4 times in every block. `slot_ids`: within one block, two choices that name the same expert have different slots. `old_place`: each expert number appears once. `new_place`: each expert number appears once.
All inputs are finite; a program needn't handle non-finite values.
Results may differ from a plain program's by a relative error of at most 0.02.
Values may be sent and summed in bfloat16 or wider, within the bound.
A program may use at most 128 MiB of HBM per device.

v0:
```python
import jax
import jax.numpy as jnp
from jax import lax
from jax.sharding import PartitionSpec as P


def placement_order(old_place, new_place):
    slot_total = old_place.shape[0]
    matches = (new_place[:, None] == old_place[None, :]).astype(jnp.int32)
    return jnp.sum(matches * jnp.arange(slot_total, dtype=jnp.int32)[None, :], axis=1)


def swiglu_rows(row_block, pair_weight):
    gate_up = jnp.einsum("rd,gud->rgu", row_block, pair_weight, preferred_element_type=jnp.float32)
    return (jax.nn.silu(gate_up[:, 0]) * gate_up[:, 1]).astype(jnp.bfloat16)


def local(
    tokens, gate_up_weight, down_weight, expert_ids, slot_ids, gate_values, old_place, new_place
):
    experts = gate_up_weight.shape[0]
    sliver = gate_up_weight.shape[2]
    model_width = tokens.shape[1]
    tok_rows = tokens.shape[0]
    choices_per_token = expert_ids.shape[1]
    capacity = 2 * tok_rows * choices_per_token // experts
    cell_count = experts * capacity
    data_ways = lax.axis_size("dp")
    slot_order = placement_order(old_place, new_place)
    cell_ids = expert_ids * capacity + slot_ids
    cell_range = jnp.arange(cell_count, dtype=jnp.int32)
    cell_hits = (cell_ids[:, :, None] == cell_range[None, None, :]).astype(jnp.float32)
    token_picks = jnp.sum(cell_hits, axis=1)
    dispatched = jnp.dot(
        token_picks.T.astype(jnp.bfloat16), tokens, preferred_element_type=jnp.float32
    ).astype(jnp.bfloat16)
    received = lax.all_to_all(
        dispatched.reshape(experts, capacity, model_width),
        "expert",
        split_axis=0,
        concat_axis=0,
        tiled=True,
    )
    own_rows = received.reshape(cell_count, model_width)
    sectioned_in = gate_up_weight.reshape(experts, 2, data_ways, sliver // data_ways, model_width)
    sectioned_down = down_weight.reshape(experts, 1, data_ways, sliver // data_ways, model_width)
    sectioned_in = jnp.take(sectioned_in, slot_order, axis=0)
    sectioned_down = jnp.take(sectioned_down, slot_order, axis=0)
    relaid_in, relaid_down = (
        lax.all_to_all(
            lax.all_to_all(sectioned_in, "dp", split_axis=2, concat_axis=3, tiled=True),
            "expert",
            split_axis=0,
            concat_axis=3,
            tiled=True,
        ),
        lax.all_to_all(
            lax.all_to_all(sectioned_down, "dp", split_axis=2, concat_axis=3, tiled=True),
            "expert",
            split_axis=0,
            concat_axis=3,
            tiled=True,
        ),
    )
    full_in, full_down = (
        lax.all_gather(relaid_in, "dp", axis=3, tiled=True),
        lax.all_gather(relaid_down, "dp", axis=3, tiled=True),
    )
    pair_in = full_in.reshape(2, -1, model_width)
    pair_down = full_down.reshape(-1, model_width)
    group_rows = lax.all_gather(own_rows, "shard", axis=0, tiled=True)
    summed = lax.psum_scatter(
        jnp.dot(
            swiglu_rows(group_rows, pair_in), pair_down, preferred_element_type=jnp.float32
        ).astype(jnp.bfloat16),
        "shard",
        scatter_dimension=0,
        tiled=True,
    )
    returned = lax.all_to_all(
        summed.reshape(experts, capacity, model_width),
        "expert",
        split_axis=0,
        concat_axis=0,
        tiled=True,
    )
    combine_weights = jnp.sum(cell_hits * gate_values[:, :, None], axis=1)
    mixed_out = jnp.dot(
        combine_weights,
        returned.reshape(cell_count, model_width).astype(jnp.float32),
        precision=lax.Precision.HIGHEST,
    )
    return mixed_out.astype(jnp.bfloat16)


def solution(mesh):
    in_specs = (
        P(("dp", "expert", "shard"), None),
        P(None, None, ("dp", "expert", "shard"), None),
        P(None, ("dp", "expert", "shard"), None),
        P(("dp", "expert", "shard"), None),
        P(("dp", "expert", "shard"), None),
        P(("dp", "expert", "shard"), None),
        P(),
        P(),
    )
    out_specs = P(("dp", "expert", "shard"), None)
    return jax.shard_map(local, mesh=mesh, in_specs=in_specs, out_specs=out_specs, check_vma=False)
```

profile of v0, /device:TPU:8, one launch (start us, length us, event | category | flops | bytes accessed | tf_op | source)
XLA Modules:
  0.0 681.6 jit_solution(10519561180992360223)
XLA Ops:
  6.5 0.0 copy-start
  6.5 0.8 multiply_add_fusion
  7.4 0.9 convert_reduce_fusion
  8.3 1.2 convolution_convert_fusion.1
  9.5 0.9 reshape.64
  10.4 8.5 %all-to-all-start = ((bf16[8,4,6144]{2,1,0:T(4,128)(2,1)}), bf16[8,4,6144]{2,1,0:T(4,128)(2,1)S(1)}, u32[]{:S(2)}, u32[]{:S(2)}) async-start(bf16[8,4,6144]{2,1,0:T(4,128)(2,1)} %reshape.64), calls=%async_computation | async-start | bytes 786432 | tf_op jit(solution)/shard_map/all_to_all | solution.py:37
  18.8 0.9 select_reduce_fusion.1
  19.7 6.4 gather_fusion
  26.1 3.5 broadcast_select_fusion
  29.6 3.1 copy.24
  32.6 0.9 all-to-all-done
  33.5 6.3 all-to-all-start.1
  39.8 0.0 all-gather.4.cloned.1.call-start
  39.9 0.9 reshape.65
  40.7 0.0 all-gather.4.cloned.1.call-update
  40.8 0.0 all-gather.6.cloned.1.call-start
  40.8 89.5 %all-to-all-done.1 = bf16[8,2,2,16,6144]{4,3,1,0,2:T(8,128)(2,1)} async-done(((bf16[8,2,2,16,6144]{4,3,1,0,2:T(8,128)(2,1)}), bf16[8,2,2,16,6144]{4,3,1,0,2:T(8,128)(2,1)}, u32[]{:S(2)}, u32[]{:S(2)}) %all-to-all-start.1) | async-done | bytes 6291488 | tf_op jit(solution)/shard_map/all_to_all | solution.py:51
  130.3 3.5 copy.25
  133.8 145.8 %all_to_all.64 = bf16[8,2,1,32,6144]{4,3,1,2,0:T(8,128)(2,1)S(1)} all-to-all(bf16[8,2,1,32,6144]{4,3,1,2,0:T(8,128)(2,1)S(1)} %bitcast.37), channel_id=1, replica_groups=mesh['dp'=2,'expert'=8,'shard'=16] {'expert'}, dimensions={0} | all-to-all | bytes 12582912 | tf_op jit(solution)/shard_map/all_to_all | solution.py:50
  279.7 3.1 copy.27
  282.8 0.0 all-gather.6.cloned.1.call-update
  282.8 0.0 all-gather.8.cloned.1.call-start
  282.8 0.0 copy-done
  282.8 2.4 gather_fusion.1
  285.3 2.3 bitcast_select_fusion
  287.5 0.3 copy.28
  287.9 63.1 %all_to_all.65 = bf16[8,1,2,16,6144]{4,3,0,1,2:T(8,128)(2,1)S(1)} all-to-all(bf16[8,1,2,16,6144]{4,3,0,1,2:T(8,128)(2,1)S(1)} %copy.28), channel_id=1, replica_groups=mesh['dp'=2,'expert'=8,'shard'=16] {'dp'}, dimensions={2} | all-to-all | bytes 6291456 | tf_op jit(solution)/shard_map/all_to_all | solution.py:58
  350.9 0.3 copy.29
  351.2 66.1 %all_to_all.66 = bf16[8,1,1,32,6144]{4,3,2,1,0:T(8,128)(2,1)} all-to-all(bf16[8,1,1,32,6144]{4,3,2,1,0:T(8,128)(2,1)S(1)} %bitcast.40), channel_id=1, replica_groups=mesh['dp'=2,'expert'=8,'shard'=16] {'expert'}, dimensions={0} | all-to-all | bytes 6291456 | tf_op jit(solution)/shard_map/all_to_all | solution.py:57
  417.4 0.0 all-gather.8.cloned.1.call-update
  417.4 0.0 reduce-scatter.2.cloned.1.call-start
  417.5 0.0 all-gather.4.cloned.1.call-done
  417.5 41.2 %all-gather.6.cloned.1.call-done = bf16[1,2,1,512,6144]{4,3,1,2,0:T(8,128)(2,1)} async-done(((bf16[1,2,1,256,6144]{4,3,1,2,0:T(8,128)(2,1)}), bf16[1,2,1,512,6144]{4,3,1,2,0:T(8,128)(2,1)}) %all-gather.6.cloned.1.call-update) | async-done | bytes 12582928 | tf_op jit(solution)/shard_map/all_gather | solution.py:66
  458.6 12.5 %fusion = f32[512,2,512]{2,0,1:T(8,128)} fusion(bf16[1,2,1,512,6144]{4,3,1,2,0:T(8,128)(2,1)} %all-gather.6.cloned.1.call-done, bf16[512,6144]{1,0:T(8,128)(2,1)} %all-gather.4.cloned.1.call-done), kind=kOutput, calls=%fused_computation.2 | convolution fusion | flops 6442450944 | bytes 20971520 | tf_op jit(solution)/shard_map/rd,gud->rgu/dot_general | solution.py:14
  471.2 72.6 %all-gather.8.cloned.1.call-done = bf16[1,1,1,512,6144]{4,3,2,1,0:T(8,128)(2,1)} async-done(((bf16[1,1,1,256,6144]{4,3,2,1,0:T(8,128)(2,1)}), bf16[1,1,1,512,6144]{4,3,2,1,0:T(8,128)(2,1)}) %all-gather.8.cloned.1.call-update) | async-done | bytes 6291472 | tf_op jit(solution)/shard_map/all_gather | solution.py:67
  543.8 0.0 copy-start.1
  543.8 9.7 %convolution_convert_fusion = bf16[512,6144]{1,0:T(8,128)(2,1)} fusion(bf16[1,1,1,512,6144]{4,3,2,1,0:T(8,128)(2,1)} %all-gather.8.cloned.1.call-done, f32[512,2,512]{2,0,1:T(8,128)} %fusion), kind=kOutput, calls=%fused_computation.4 | convolution fusion | flops 3225944064 | bytes 14680064 | tf_op jit(solution)/shard_map/dot_general | solution.py:73
  553.5 0.0 reduce-scatter.2.cloned.1.call-update
  553.6 98.3 %reduce-scatter.2.cloned.1.call-done = bf16[32,6144]{1,0:T(8,128)(2,1)} async-done(((bf16[512,6144]{1,0:T(8,128)(2,1)}), bf16[32,6144]{1,0:T(8,128)(2,1)}) %reduce-scatter.2.cloned.1.call-update) | async-done | bytes 393232 | tf_op jit(solution)/shard_map/reduce_scatter | solution.py:72
  651.9 1.1 reshape.70
  653.0 20.0 %all_to_all.67 = bf16[8,4,6144]{2,1,0:T(4,128)(2,1)} all-to-all(bf16[8,4,6144]{2,1,0:T(4,128)(2,1)S(1)} %reshape.70), channel_id=1, replica_groups=mesh['dp'=2,'expert'=8,'shard'=16] {'expert'}, dimensions={0} | all-to-all | bytes 786432 | tf_op jit(solution)/shard_map/all_to_all | solution.py:80
  673.1 1.1 reshape.71
  674.1 0.9 convolution_convert_fusion.2
  675.1 0.0 copy-done.1
  (3 shorter events, 0.0 us)
Async XLA Ops:
  6.5 276.3 %copy-start = (bf16[8,32,6144]{2,1,0:T(8,128)(2,1)S(1)}, bf16[8,32,6144]{2,1,0:T(8,128)(2,1)}, u32[]{:S(2)}) copy-start(bf16[8,32,6144]{2,1,0:T(8,128)(2,1)} %param.10) | copy-start | bytes 9437188
  10.4 23.2 %all-to-all-start = ((bf16[8,4,6144]{2,1,0:T(4,128)(2,1)}), bf16[8,4,6144]{2,1,0:T(4,128)(2,1)S(1)}, u32[]{:S(2)}, u32[]{:S(2)}) async-start(bf16[8,4,6144]{2,1,0:T(4,128)(2,1)} %reshape.64), calls=%async_computation | async-start | bytes 786432 | tf_op jit(solution)/shard_map/all_to_all | solution.py:37
  33.5 96.8 %all-to-all-start.1 = ((bf16[8,2,2,16,6144]{4,3,1,0,2:T(8,128)(2,1)}), bf16[8,2,2,16,6144]{4,3,1,0,2:T(8,128)(2,1)}, u32[]{:S(2)}, u32[]{:S(2)}) async-start(bf16[8,2,2,16,6144]{4,3,1,0,2:T(8,128)(2,1)} %copy.24), calls=%async_computation.1 | async-start | bytes 12582912 | tf_op jit(solution)/shard_map/all_to_all | solution.py:51
  39.8 377.6 %all-gather.4.cloned.1.call-start = ((), (), s32[]{:S(2)}) async-start(), calls=%async_computation.7 | async-start | bytes 6684672 | tf_op jit(solution)/shard_map/all_gather | solution.py:71
  40.8 417.9 %all-gather.6.cloned.1.call-start = ((), (), s32[]{:S(2)}) async-start(), calls=%async_computation.8 | async-start | bytes 18874368 | tf_op jit(solution)/shard_map/all_gather | solution.py:66
  282.8 261.0 %all-gather.8.cloned.1.call-start = ((), (), s32[]{:S(2)}) async-start(), calls=%async_computation.9 | async-start | bytes 9437184 | tf_op jit(solution)/shard_map/all_gather | solution.py:67
  417.4 234.5 %reduce-scatter.2.cloned.1.call-start = ((), (), s32[]{:S(2)}) async-start(), calls=%async_computation.10 | async-start | bytes 6684672 | tf_op jit(solution)/shard_map/reduce_scatter | solution.py:72
  543.8 131.2 %copy-start.1 = (bf16[8,32,6144]{2,1,0:T(8,128)(2,1)S(1)}, bf16[8,32,6144]{2,1,0:T(8,128)(2,1)}, u32[]{:S(2)}) copy-start(bf16[8,32,6144]{2,1,0:T(8,128)(2,1)} %param.10) | copy-start | bytes 9437188
Sparse Core Ops, SparseCore 0:
  43.4 90.1 all-gather.3
  282.9 175.6 all-gather.5
  460.4 83.3 all-gather.7
  553.7 98.1 reduce-scatter.1
where the time goes:
time: 682 us
  waiting for transfers between devices  303 us (44%)
  blocking collectives  295 us (43%)
  matrix products  24.3 us (4%)
  local copies, waits for them, and re-layouts  23.1 us (3%)
  starting transfers between devices  15 us (2%)
  between operations  13.2 us (2%)
  other arithmetic  8.31 us (1%)
    all_to_all x1, blocking collectives, local(): lax.all_to_all(lax.all_to_all(sectioned_in, 'dp', split_axis=2, concat_ax...  146 us
    reduce_scatter x1, waiting for transfers between devices, local(): lax.psum_scatter(jnp.dot(swiglu_rows(group_rows, pair_in), pair_down, pre...  98.3 us
    all_to_all x1, waiting for transfers between devices, local(): lax.all_to_all(sectioned_in, 'dp', split_axis=2, concat_axis=3, tiled=True)  89.5 us
    all_gather x1, waiting for transfers between devices, local(): lax.all_gather(relaid_down, 'dp', axis=3, tiled=True)  72.6 us
    all_to_all x1, blocking collectives, local(): lax.all_to_all(lax.all_to_all(sectioned_down, 'dp', split_axis=2, concat_...  66.1 us
    all_to_all x1, blocking collectives, local(): lax.all_to_all(sectioned_down, 'dp', split_axis=2, concat_axis=3, tiled=T...  63.1 us
    all_gather x1, waiting for transfers between devices, local(): lax.all_gather(relaid_in, 'dp', axis=3, tiled=True)  41.2 us
    all_to_all x1, blocking collectives, local(): lax.all_to_all(summed.reshape(experts, capacity, model_width), 'expert',...  20 us
  transfers between devices with their start and end apart: 6, of which 5 were waited for; matrix products, arithmetic and copies ran while one was open for 6% of the time, Pallas kernels for 0%

commit v1 on v0

--- a/solution.py
+++ b/solution.py
@@ -63,7 +63,7 @@
         ),
     )
     full_in, full_down = (
-        lax.all_gather(relaid_in, "dp", axis=3, tiled=True),
+        jnp.concatenate(lax.all_gather(relaid_in, "dp"), axis=3),
         lax.all_gather(relaid_down, "dp", axis=3, tiled=True),
     )
     pair_in = full_in.reshape(2, -1, model_width)

time: 682 us -> 727 us (1.066)
  blocking collectives: 295 us -> 402 us
  waiting for transfers between devices: 303 us -> 249 us
  starting transfers between devices: 15 us -> 0.13 us
  local copies, waits for them, and re-layouts: 23.1 us -> 30.6 us
    all_to_all x2 -> x0, waiting for transfers between devices: 90.4 us -> none  [the longest x1 89.5 us: local(): lax.all_to_all(sectioned_in, 'dp', split_axis=2, concat_axis=3, tiled=True)]
    all_to_all x0 -> x2, blocking collectives: none -> 88.4 us  [the longest x1 73 us: local(): lax.all_to_all(sectioned_in, 'dp', split_axis=2, concat_axis=3, tiled=True)]
    all_gather x1, waiting for transfers between devices: 0.02 us -> 60.5 us  [local(): group_rows = lax.all_gather(own_rows, 'shard', axis=0, tiled=True)]
    all_gather x1, waiting for transfers between devices: 41.2 us -> 16.4 us  [local(): lax.all_gather(relaid_in, 'dp')]
    all_to_all x2 -> x0, starting transfers between devices: 14.8 us -> none  [the longest x1 8.47 us: local(): lax.all_to_all(dispatched.reshape(experts, capacity, model_width), 'exper...]
    reshape x0 -> x1, local copies, waits for them, and re-layouts: none -> 10.7 us  [local(): jnp.concatenate(lax.all_gather(relaid_in, 'dp'), axis=3)]
    all_to_all x1, blocking collectives: 63.1 us -> 72.3 us  [local(): lax.all_to_all(sectioned_down, 'dp', split_axis=2, concat_axis=3, tiled=T...]
  transfers between devices with their start and end apart: 6 -> 4, of which waited for: 5 -> 4; matrix products, arithmetic and copies ran while one was open for 6% -> 5% of each run, Pallas kernels for 0% -> 0%
where the time goes in v1:
time: 727 us; the launch traced here: 726 us
  blocking collectives  402 us (55%)
  waiting for transfers between devices  249 us (34%)
  local copies, waits for them, and re-layouts  30.6 us (4%)
  matrix products  24.2 us (3%)
  between operations  13.2 us (2%)
    all_to_all x1, blocking collectives, local(): lax.all_to_all(lax.all_to_all(sectioned_in, 'dp', split_axis=2, concat_ax...  148 us
    reduce_scatter x1, waiting for transfers between devices, local(): lax.psum_scatter(jnp.dot(swiglu_rows(group_rows, pair_in), pair_down, pre...  98.3 us
    all_gather x1, waiting for transfers between devices, local(): lax.all_gather(relaid_down, 'dp', axis=3, tiled=True)  73.9 us
    all_to_all x1, blocking collectives, local(): lax.all_to_all(sectioned_in, 'dp', split_axis=2, concat_axis=3, tiled=True)  73 us
    all_to_all x1, blocking collectives, local(): lax.all_to_all(lax.all_to_all(sectioned_down, 'dp', split_axis=2, concat_...  72.9 us
    all_to_all x1, blocking collectives, local(): lax.all_to_all(sectioned_down, 'dp', split_axis=2, concat_axis=3, tiled=T...  72.3 us
    all_gather x1, waiting for transfers between devices, local(): group_rows = lax.all_gather(own_rows, 'shard', axis=0, tiled=True)  60.5 us
    all_to_all x1, blocking collectives, local(): lax.all_to_all(summed.reshape(experts, capacity, model_width), 'expert',...  20 us
  transfers between devices with their start and end apart: 4, of which 4 were waited for; matrix products, arithmetic and copies ran while one was open for 5% of the time, Pallas kernels for 0%

profile of v1, /device:TPU:8, one launch (start us, length us, event | category | flops | bytes accessed | tf_op | source)
XLA Modules:
  0.0 726.5 jit_solution(12490034898772001527)
XLA Ops:
  6.5 0.0 copy-start
  6.5 0.0 all-gather.6.cloned.1.call-start
  6.5 1.0 select_reduce_fusion.1
  7.6 6.4 gather_fusion
  14.0 3.5 broadcast_select_fusion
  17.4 0.7 copy.35
  18.2 73.0 %all_to_all.61 = bf16[8,2,2,16,6144]{4,3,1,0,2:T(8,128)(2,1)S(1)} all-to-all(bf16[8,2,2,16,6144]{4,3,1,0,2:T(8,128)(2,1)S(1)} %copy.35), channel_id=1, replica_groups=mesh['dp'=2,'expert'=8,'shard'=16] {'dp'}, dimensions={2} | all-to-all | bytes 12582912 | tf_op jit(solution)/shard_map/all_to_all | solution.py:51
  91.1 0.7 copy.36
  91.9 148.5 %all_to_all.62 = bf16[8,2,1,32,6144]{4,3,1,2,0:T(8,128)(2,1)S(1)} all-to-all(bf16[8,2,1,32,6144]{4,3,1,2,0:T(8,128)(2,1)S(1)} %bitcast.40), channel_id=1, replica_groups=mesh['dp'=2,'expert'=8,'shard'=16] {'expert'}, dimensions={0} | all-to-all | bytes 12582912 | tf_op jit(solution)/shard_map/all_to_all | solution.py:50
  240.4 3.0 copy.38
  243.4 0.0 copy-start.3
  243.4 0.0 copy-start.4
  243.4 0.0 copy-start.5
  243.4 0.0 copy-start.2
  243.4 0.0 all-gather.6.cloned.1.call-update
  243.4 0.0 all-gather.4.cloned.1.call-start
  243.5 0.6 copy-done.3
  244.1 0.0 copy-done.4
  244.1 0.0 copy-done.5
  244.1 0.1 convert_reduce_fusion
  244.2 0.2 copy-done.2
  244.3 1.0 convolution_convert_fusion.1
  245.4 1.1 reshape.65
  246.5 15.4 %all_to_all.63 = bf16[8,4,6144]{2,1,0:T(4,128)(2,1)} all-to-all(bf16[8,4,6144]{2,1,0:T(4,128)(2,1)S(1)} %reshape.65), channel_id=1, replica_groups=mesh['dp'=2,'expert'=8,'shard'=16] {'expert'}, dimensions={0} | all-to-all | bytes 786432 | tf_op jit(solution)/shard_map/all_to_all | solution.py:37
  261.9 1.9 reshape.66
  263.8 0.0 all-gather.4.cloned.1.call-update
  263.8 0.0 all-gather.8.cloned.1.call-start
  263.9 0.0 copy-done
  263.9 2.4 gather_fusion.1
  266.3 2.6 bitcast_select_fusion
  268.9 0.3 copy.41
  269.2 72.3 %all_to_all.64 = bf16[8,1,2,16,6144]{4,3,0,1,2:T(8,128)(2,1)S(1)} all-to-all(bf16[8,1,2,16,6144]{4,3,0,1,2:T(8,128)(2,1)S(1)} %copy.41), channel_id=1, replica_groups=mesh['dp'=2,'expert'=8,'shard'=16] {'dp'}, dimensions={2} | all-to-all | bytes 6291456 | tf_op jit(solution)/shard_map/all_to_all | solution.py:58
  341.5 0.3 copy.42
  341.8 72.9 %all_to_all.65 = bf16[8,1,1,32,6144]{4,3,2,1,0:T(8,128)(2,1)} all-to-all(bf16[8,1,1,32,6144]{4,3,2,1,0:T(8,128)(2,1)S(1)} %bitcast.44), channel_id=1, replica_groups=mesh['dp'=2,'expert'=8,'shard'=16] {'expert'}, dimensions={0} | all-to-all | bytes 6291456 | tf_op jit(solution)/shard_map/all_to_all | solution.py:57
  414.6 0.0 all-gather.8.cloned.1.call-update
  414.7 0.0 reduce-scatter.2.cloned.1.call-start
  414.7 16.4 %all-gather.6.cloned.1.call-done = bf16[2,1,2,1,256,6144]{5,4,3,2,1,0:T(8,128)(2,1)} async-done(((bf16[1,1,2,1,256,6144]{5,4,3,2,1,0:T(8,128)(2,1)}), bf16[2,1,2,1,256,6144]{5,4,3,2,1,0:T(8,128)(2,1)}) %all-gather.6.cloned.1.call-update) | async-done | bytes 12582928 | tf_op jit(solution)/shard_map/all_gather | solution.py:66
  431.1 10.7 %copy.40 = bf16[1,2,1,2,256,6144]{5,4,3,1,2,0:T(8,128)(2,1)} copy(bf16[1,2,1,2,256,6144]{5,4,2,1,0,3:T(8,128)(2,1)} %bitcast.41) | data formatting | bytes 25165824 | tf_op jit(solution)/shard_map/reshape | solution.py:66
  441.8 60.5 %all-gather.4.cloned.1.call-done = bf16[512,6144]{1,0:T(8,128)(2,1)} async-done(((bf16[32,6144]{1,0:T(8,128)(2,1)}), bf16[512,6144]{1,0:T(8,128)(2,1)}) %all-gather.4.cloned.1.call-update) | async-done | bytes 6291472 | tf_op jit(solution)/shard_map/all_gather | solution.py:71
  502.3 12.5 %fusion.1 = f32[512,2,512]{2,0,1:T(8,128)} fusion(bf16[2,512,6144]{2,1,0:T(8,128)(2,1)} %bitcast.42, bf16[512,6144]{1,0:T(8,128)(2,1)} %all-gather.4.cloned.1.call-done), kind=kOutput, calls=%fused_computation.6 | convolution fusion | flops 6442450944 | bytes 20971520 | tf_op jit(solution)/shard_map/rd,gud->rgu/dot_general | solution.py:14
  514.8 73.9 %all-gather.8.cloned.1.call-done = bf16[1,1,1,512,6144]{4,3,2,1,0:T(8,128)(2,1)} async-done(((bf16[1,1,1,256,6144]{4,3,2,1,0:T(8,128)(2,1)}), bf16[1,1,1,512,6144]{4,3,2,1,0:T(8,128)(2,1)}) %all-gather.8.cloned.1.call-update) | async-done | bytes 6291472 | tf_op jit(solution)/shard_map/all_gather | solution.py:67
  588.7 0.0 copy-start.1
  588.7 9.7 %convolution_convert_fusion = bf16[512,6144]{1,0:T(8,128)(2,1)} fusion(bf16[1,1,1,512,6144]{4,3,2,1,0:T(8,128)(2,1)} %all-gather.8.cloned.1.call-done, f32[512,2,512]{2,0,1:T(8,128)} %fusion.1), kind=kOutput, calls=%fused_computation.2 | convolution fusion | flops 3225944064 | bytes 14680064 | tf_op jit(solution)/shard_map/dot_general | solution.py:73
  598.4 0.0 reduce-scatter.2.cloned.1.call-update
  598.4 98.3 %reduce-scatter.2.cloned.1.call-done = bf16[32,6144]{1,0:T(8,128)(2,1)} async-done(((bf16[512,6144]{1,0:T(8,128)(2,1)}), bf16[32,6144]{1,0:T(8,128)(2,1)}) %reduce-scatter.2.cloned.1.call-update) | async-done | bytes 393232 | tf_op jit(solution)/shard_map/reduce_scatter | solution.py:72
  696.8 1.1 reshape.71
  697.9 20.0 %all_to_all.66 = bf16[8,4,6144]{2,1,0:T(4,128)(2,1)} all-to-all(bf16[8,4,6144]{2,1,0:T(4,128)(2,1)S(1)} %reshape.71), channel_id=1, replica_groups=mesh['dp'=2,'expert'=8,'shard'=16] {'expert'}, dimensions={0} | all-to-all | bytes 786432 | tf_op jit(solution)/shard_map/all_to_all | solution.py:80
  717.9 1.1 reshape.72
  719.0 0.9 convolution_convert_fusion.2
  719.9 0.0 copy-done.1
  (4 shorter events, 0.0 us)
Async XLA Ops:
  6.5 257.3 %copy-start = (bf16[8,32,6144]{2,1,0:T(8,128)(2,1)S(1)}, bf16[8,32,6144]{2,1,0:T(8,128)(2,1)}, u32[]{:S(2)}) copy-start(bf16[8,32,6144]{2,1,0:T(8,128)(2,1)} %param.10) | copy-start | bytes 9437188
  6.5 424.6 %all-gather.6.cloned.1.call-start = ((), (), s32[]{:S(2)}) async-start(), calls=%async_computation.8 | async-start | bytes 18874368 | tf_op jit(solution)/shard_map/all_gather | solution.py:66
  243.4 0.7 copy-start.3
  243.4 0.7 copy-start.4
  243.4 0.7 copy-start.5
  243.4 0.9 copy-start.2
  243.4 258.9 %all-gather.4.cloned.1.call-start = ((), (), s32[]{:S(2)}) async-start(), calls=%async_computation.7 | async-start | bytes 6684672 | tf_op jit(solution)/shard_map/all_gather | solution.py:71
  263.8 324.9 %all-gather.8.cloned.1.call-start = ((), (), s32[]{:S(2)}) async-start(), calls=%async_computation.9 | async-start | bytes 9437184 | tf_op jit(solution)/shard_map/all_gather | solution.py:67
  414.7 282.1 %reduce-scatter.2.cloned.1.call-start = ((), (), s32[]{:S(2)}) async-start(), calls=%async_computation.10 | async-start | bytes 6684672 | tf_op jit(solution)/shard_map/reduce_scatter | solution.py:72
  588.7 131.2 %copy-start.1 = (bf16[8,32,6144]{2,1,0:T(8,128)(2,1)S(1)}, bf16[8,32,6144]{2,1,0:T(8,128)(2,1)}, u32[]{:S(2)}) copy-start(bf16[8,32,6144]{2,1,0:T(8,128)(2,1)} %param.10) | copy-start | bytes 9437188
Sparse Core Ops, SparseCore 0:
  243.5 187.5 all-gather.5
  433.9 68.3 all-gather.3
  504.1 84.5 all-gather.7
  598.6 98.1 reduce-scatter.1
